TPU v7x, 32 devices: a whole 2x2x4 slice. The times are simulated.
32 devices in a mesh: reg: 16 (over z, y, x), col: 2 (over core).
Axes of the slice: x: 2, y: 2, z: 4, core: 2. Of those that a mesh axis runs over, the one named last changes fastest.
Arguments:
- innovation: float32 [64, 131072], P(None, ('reg', 'col')), may hold values from -6 to 6
- obs_along: float32 [131072], P(('reg', 'col')), may hold values from 0 to 2
- obs_across: float32 [131072], P(('reg', 'col')), may hold values from 0 to 32
- obs_scale: float32 [131072], P(('reg', 'col')), may hold values from 0.5 to 2
- obs_error: float32 [131072], P(('reg', 'col')), may hold values from 0.1 to 1
- obs_gain: float32 [131072], P(('reg', 'col')), may hold values from 0.3 to 3
- pair_live: int32 [128, 2], P(('reg', 'col')), may hold values 0 or 1
- obs_count: int32 [128], P(('reg', 'col')), may hold values from 256 to 1024, as said below
- col_owner: int32 [131072], P(('reg', 'col')), may hold values from 0 to 32767, as said below
Outputs:
- weights: float32 [64, 131072], P(None, ('reg', 'col'))
- increments: float32 [64, 32768], P(None, ('reg', 'col'))
Inputs may be any that keep to these rules, and one draw needn't show every extreme that they name: `obs_count`: slots of a region block at or after its count are empty. Some region holds 1024 observations and some holds 256. `col_owner`: observation slot o lies in device block k = o // 4096, and its column is one of k * 1024 to k * 1024 + 2 * 1024 - 1, taken modulo 32768; column block k belongs to the same position k in the order of devices.
All inputs are finite; a program needn't handle non-finite values. No bound on the sum of `pair_live` on one device may be relied on, other than what follows from the above.
Results may differ from a plain program's by a relative error of at most 0.0003.
Values sent between devices are 32-bit elements; how exact they have to be, the bound alone decides.
A program may use at most 64 MiB of HBM per device.

v0:
```python
import functools

import jax
import jax.numpy as jnp
from jax import lax
from jax.experimental import pallas as pl
from jax.experimental.pallas import tpu as pltpu
from jax.sharding import PartitionSpec as P

ROWS = 1024
REACH = 2
COLS_DEV = 1024
META = 16
KB = 128
NB = 128
UNROLL = 4
DEAD = 1e9
VMEM_LIMIT = 60 * 1024 * 1024

highest = lax.Precision.HIGHEST
f32 = jnp.float32
bf16 = jnp.bfloat16
NT = (((1,), (1,)), ((), ()))
NN = (((1,), (0,)), ((), ()))
TN = (((0,), (0,)), ((), ()))
vmem = pl.BlockSpec(memory_space=pltpu.VMEM)
smem = pl.BlockSpec(memory_space=pltpu.SMEM)


def shift(block, distance):
    axis = ("reg", "col")
    n = lax.axis_size(axis)
    return lax.ppermute(block, axis, [((i - distance) % n, i) for i in range(n)])


def dot(a, b, dims=NN):
    return lax.dot_general(a, b, dims, preferred_element_type=f32)


def two(x):
    hi = x.astype(bf16)
    return hi, (x - hi.astype(f32)).astype(bf16)


def three(x):
    hi = x.astype(bf16)
    rest = x - hi.astype(f32)
    mid = rest.astype(bf16)
    return hi, mid, (rest - mid.astype(f32)).astype(bf16)


def combine(coef_t, blocks):
    chi, clo = two(coef_t)
    bhi, blo = two(blocks)
    return dot(
        jnp.concatenate([chi, chi, clo], axis=1), jnp.concatenate([bhi, blo, bhi], axis=0)
    )


def params():
    return pltpu.CompilerParams(vmem_limit_bytes=VMEM_LIMIT)


def sort_kernel(innov_ref, meta_ref, first_ref, last_ref, rank_ref):
    regions = innov_ref.shape[1] // ROWS
    kept = first_ref.shape[0]
    sub = lax.broadcasted_iota(jnp.int32, (ROWS, 128), 0)
    lane = lax.broadcasted_iota(jnp.int32, (ROWS, 128), 1)
    for g in range(regions):
        cols = pl.ds(g * ROWS, ROWS)
        meta = meta_ref[:, cols]
        key = meta[6:7]
        live = (key < 0.5 * DEAD).astype(f32)
        key_col = jnp.broadcast_to(key, (128, ROWS)).T
        ranks = []
        for b in range(ROWS // 128):
            mine = key[:, b * 128 : (b + 1) * 128]
            before = (key_col < mine) | ((key_col == mine) & (sub < lane + b * 128))
            ranks.append(jnp.sum(before.astype(f32), axis=0, keepdims=True))
        rank = jnp.concatenate(ranks, axis=1)
        rank_ref[:, cols] = jnp.broadcast_to(rank, (8, ROWS))
        stack = jnp.concatenate([innov_ref[:, cols] * live, meta], axis=0)
        lhs = jnp.concatenate(three(stack), axis=0)
        n = stack.shape[0]
        rank_i = rank.astype(jnp.int32)
        out_ref = first_ref if g < regions // 2 else last_ref
        for c in range(ROWS // 256):
            slot = lax.broadcasted_iota(jnp.int32, (256, ROWS), 0) + c * 256
            place = (slot == rank_i).astype(f32).astype(bf16)
            got = dot(lhs, place, NT)
            start = (g % (regions // 2)) * ROWS + c * 256
            out_ref[:, start : start + 256] = (got[:n] + got[n : 2 * n] + got[2 * n :])[:kept]


def sort_call(innov, meta):
    ens, n = innov.shape
    half = jax.ShapeDtypeStruct((ens + 8, n // 2), f32)
    return pl.pallas_call(
        sort_kernel,
        out_shape=(half, half, jax.ShapeDtypeStruct((8, n), f32)),
        in_specs=[vmem, vmem],
        out_specs=(vmem, vmem, vmem),
        compiler_params=params(),
        name="sort_slots",
    )(innov, meta)


def build_list(bounds_ref, list_ref, tile_ref, count_ref, tiles):
    per = ROWS // NB
    zero_block = (tiles // per + 2 * REACH) * (ROWS // KB)

    def one(t, trip):
        g = t // per
        base = trip * UNROLL

        def put(dh, jb, n):
            list_ref[n] = (g + dh) * (ROWS // KB) + jb
            return n + 1

        n = base
        for dh in range(2 * REACH + 1):
            lo = bounds_ref[0, dh * tiles + t]
            hi = bounds_ref[1, dh * tiles + t]
            n = lax.fori_loop(lo, hi, functools.partial(put, dh), n)
        for p in range(UNROLL):
            list_ref[n + p] = zero_block
        end = (n + UNROLL - 1) // UNROLL

        def mark(k, carry):
            tile_ref[k] = t
            return carry

        lax.fori_loop(trip, end, mark, 0)
        return end

    trips = lax.fori_loop(0, tiles, one, 0)
    tile_ref[trips] = 0
    for p in range(UNROLL):
        list_ref[trips * UNROLL + p] = zero_block
    count_ref[0] = trips


def prepare(chunks, row_ref, along_ref, across_ref):
    width = chunks[0].shape[1]
    per = width // ROWS
    for c, ref in enumerate(chunks):
        row_ref[:, c * width : (c + 1) * width] = ref[ref.shape[0] - 8 :, :]
        for r in range(per):
            h = c * per + r
            at = slice(h * ROWS, (h + 1) * ROWS)
            row_ref[0:1, at] = row_ref[0:1, at] + float(h)
            col = row_ref[:, at].T
            along_ref[at, :] = jnp.broadcast_to(col[:, 0:1], (ROWS, NB))
            across_ref[at, :] = jnp.broadcast_to(col[:, 1:2], (ROWS, NB))
    wide = width * len(chunks)
    along_ref[wide : wide + KB, :] = jnp.zeros((KB, NB), f32)
    across_ref[wide : wide + KB, :] = jnp.zeros((KB, NB), f32)


def apply_cov(list_ref, tile_ref, count_ref, row_ref, along_ref, across_ref, v_ref, img_ref, stack_ref, s_ref):
    ens, wide = v_ref.shape
    own = img_ref.shape[1]
    lead = REACH * ROWS
    chunk = 2048
    for c in range(wide // chunk):
        at = pl.ds(c * chunk, chunk)
        hi, lo = two(v_ref[:, at] * row_ref[2:3, at])
        stack_ref[0:ens, at] = hi
        stack_ref[ens : 2 * ens, at] = lo
    stack_ref[:, wide : wide + KB] = jnp.zeros((2 * ens, KB), bf16)
    s_ref[...] = jnp.zeros_like(s_ref)
    img_ref[...] = jnp.zeros_like(img_ref)
    depth = UNROLL * KB

    def step(k, carry):
        before = jnp.maximum(k - 1, 0)
        vhi, vlo = [], []
        for p in range(UNROLL):
            block = list_ref[before * UNROLL + p]
            part = stack_ref[:, pl.ds(pl.multiple_of(block * KB, KB), KB)]
            vhi.append(part[:ens])
            vlo.append(part[ens:])
        lhs = jnp.concatenate(vhi + vlo + vhi, axis=1)
        shi = s_ref[:depth]
        rhs = jnp.concatenate([shi, shi, s_ref[depth:]], axis=0)
        o_at = pl.ds(pl.multiple_of(tile_ref[before] * NB, NB), NB)
        img_ref[:, o_at] += dot(lhs, rhs)
        i_at = pl.ds(pl.multiple_of(lead + tile_ref[k] * NB, NB), NB)
        a_i = row_ref[0:1, i_at]
        b_i = row_ref[1:2, i_at]
        for p in range(UNROLL):
            block = list_ref[k * UNROLL + p]
            j_at = pl.ds(pl.multiple_of(block * KB, KB), KB)
            da = along_ref[j_at, :] - a_i
            db = across_ref[j_at, :] - b_i
            r2 = da * da + db * db
            r = r2 * lax.rsqrt(jnp.maximum(r2, 1e-30))
            u = jnp.maximum(1.0 - r, 0.0)
            u2 = u * u
            hi, lo = two((u2 * u2) * (r + 0.25))
            s_ref[p * KB : (p + 1) * KB] = hi
            s_ref[depth + p * KB : depth + (p + 1) * KB] = lo
        return carry

    lax.fori_loop(0, count_ref[0] + 1, step, 0)
    for c in range(own // chunk):
        at = slice(c * chunk, (c + 1) * chunk)
        e_at = slice(lead + c * chunk, lead + (c + 1) * chunk)
        img_ref[:, at] = (
            img_ref[:, at] * (row_ref[2:3, e_at] * 0.25) + row_ref[3:4, e_at] * v_ref[:, e_at]
        )


def gram(a, b):
    ahi, alo = two(a)
    bhi, blo = two(b)
    return dot(
        jnp.concatenate([ahi, ahi, alo], axis=1), jnp.concatenate([bhi, blo, bhi], axis=1), NT
    )


def first_kernel(
    bounds_ref,
    c0,
    c1,
    c2,
    c3,
    imga_ref,
    imgb_ref,
    gram_ref,
    list_ref,
    tile_ref,
    count_ref,
    row_ref,
    along_ref,
    across_ref,
    v_ref,
    img_ref,
    stack_ref,
    s_ref,
):
    ens, own = img_ref.shape
    lead = REACH * ROWS
    chunks = [c0, c1, c2, c3]
    build_list(bounds_ref, list_ref, tile_ref, count_ref, own // NB)
    prepare(chunks, row_ref, along_ref, across_ref)
    for c, ref in enumerate(chunks):
        v_ref[:, c * lead : (c + 1) * lead] = ref[:ens, :]
    apply_cov(
        list_ref, tile_ref, count_ref, row_ref, along_ref, across_ref, v_ref, img_ref, stack_ref, s_ref
    )
    imga_ref[...] = img_ref[:, :lead]
    imgb_ref[...] = img_ref[:, lead:]
    r = v_ref[:, lead : lead + own]
    gram_ref[...] = gram(r, jnp.concatenate([r, img_ref[...]], axis=0))


def second_kernel(
    list_ref,
    tile_ref,
    count_ref,
    step_ref,
    c0,
    c1,
    c2,
    c3,
    i0,
    i1,
    i2,
    i3,
    gram_ref,
    row_ref,
    along_ref,
    across_ref,
    v_ref,
    img_ref,
    stack_ref,
    s_ref,
):
    ens, own = img_ref.shape
    lead = REACH * ROWS
    chunks = [c0, c1, c2, c3]
    prepare(chunks, row_ref, along_ref, across_ref)
    step_t = step_ref[...].T
    for c, (ref, image) in enumerate(zip(chunks, [i0, i1, i2, i3])):
        v_ref[:, c * lead : (c + 1) * lead] = ref[:ens, :] - combine(step_t, image[...])
    apply_cov(
        list_ref, tile_ref, count_ref, row_ref, along_ref, across_ref, v_ref, img_ref, stack_ref, s_ref
    )
    r = v_ref[:, lead : lead + own]
    gram_ref[:ens] = gram(r, jnp.concatenate([r, img_ref[...]], axis=0))
    mixed = gram(r, jnp.concatenate([i1[...], i2[...]], axis=1))
    gram_ref[ens:] = jnp.concatenate([mixed, mixed], axis=1)


def scratch(ens, own):
    wide = own + 2 * REACH * ROWS
    return [
        pltpu.VMEM((8, wide), f32),
        pltpu.VMEM((wide + KB, NB), f32),
        pltpu.VMEM((wide + KB, NB), f32),
        pltpu.VMEM((ens, wide), f32),
        pltpu.VMEM((ens, own), f32),
        pltpu.VMEM((2 * ens, wide + KB), bf16),
        pltpu.VMEM((2 * UNROLL * KB, NB), bf16),
    ]


def first_call(bounds, chunks, ens, own):
    tiles = own // NB
    trips = tiles * -(-(2 * REACH + 1) * (ROWS // KB) // UNROLL) + 2
    half = jax.ShapeDtypeStruct((ens, own // 2), f32)
    return pl.pallas_call(
        first_kernel,
        out_shape=(
            half,
            half,
            jax.ShapeDtypeStruct((ens, 2 * ens), f32),
            jax.ShapeDtypeStruct((trips * UNROLL,), jnp.int32),
            jax.ShapeDtypeStruct((trips,), jnp.int32),
            jax.ShapeDtypeStruct((1,), jnp.int32),
        ),
        in_specs=[smem] + [vmem] * 4,
        out_specs=(vmem, vmem, vmem, smem, smem, smem),
        scratch_shapes=scratch(ens, own),
        compiler_params=params(),
        name="operate_first",
    )(bounds, *chunks)


def second_call(lists, step, chunks, images, ens, own):
    return pl.pallas_call(
        second_kernel,
        out_shape=jax.ShapeDtypeStruct((2 * ens, 2 * ens), f32),
        in_specs=[smem] * 3 + [vmem] * 9,
        out_specs=vmem,
        scratch_shapes=scratch(ens, own),
        compiler_params=params(),
        name="operate_second",
    )(*lists, step, *chunks, *images)


def reduce_kernel(steps, n_col, x_ref, out_ref, send, recv, send_sem, recv_sem):
    me = lax.axis_index("reg") * n_col + lax.axis_index("col")
    partners = []
    for k in range(steps):
        size = 2**k
        other = me + size * (1 - 2 * ((me // size) % 2))
        partners.append((other // n_col, other % n_col))
    barrier = pltpu.get_barrier_semaphore()
    for other in partners:
        pl.semaphore_signal(
            barrier, inc=1, device_id=other, device_id_type=pl.DeviceIdType.MESH
        )
    pl.semaphore_wait(barrier, steps)
    total = x_ref[...]
    for k in range(steps):
        if k:
            send[k] = total
        copy = pltpu.make_async_remote_copy(
            src_ref=send.at[k] if k else x_ref,
            dst_ref=recv.at[k],
            send_sem=send_sem.at[k],
            recv_sem=recv_sem.at[k],
            device_id=partners[k],
            device_id_type=pl.DeviceIdType.MESH,
        )
        copy.start()
        copy.wait()
        total = total + recv[k]
    out_ref[...] = total


def sum_all(x, which):
    n_col = lax.axis_size("col")
    steps = (lax.axis_size("reg") * n_col).bit_length() - 1
    return pl.pallas_call(
        functools.partial(reduce_kernel, steps, n_col),
        out_shape=jax.ShapeDtypeStruct(x.shape, f32),
        in_specs=[vmem],
        out_specs=vmem,
        scratch_shapes=[
            pltpu.VMEM((steps,) + x.shape, f32),
            pltpu.VMEM((steps,) + x.shape, f32),
            pltpu.SemaphoreType.DMA((steps,)),
            pltpu.SemaphoreType.DMA((steps,)),
        ],
        compiler_params=pltpu.CompilerParams(collective_id=which, has_side_effects=True),
        name="sum_all",
    )(x)


def symmetric(matrix):
    return 0.5 * (matrix + matrix.T)


def mm(a, b, dims=NN):
    return lax.dot_general(a, b, dims, precision=highest, preferred_element_type=f32)


def eliminate(chains):
    ens, both = chains[0].shape
    rows = lax.broadcasted_iota(jnp.int32, (ens, both), 0)
    for k in range(ens):
        done = []
        for m in chains:
            col = jnp.broadcast_to(m[:, k : k + 1], (ens, both))
            pivot = m[k : k + 1] / col[k : k + 1]
            done.append(jnp.where(rows == k, pivot, m - col * pivot))
        chains = done
    return [m[:, ens:] for m in chains]


def solve_first_kernel(gram_ref, step_ref, inv_ref, curv_ref):
    ens = gram_ref.shape[0]
    norm = symmetric(gram_ref[:, :ens])
    curv = symmetric(gram_ref[:, ens:])
    rows = lax.broadcasted_iota(jnp.int32, (ens, ens), 0)
    eye = (rows == lax.broadcasted_iota(jnp.int32, (ens, ens), 1)).astype(f32)
    step, inv = eliminate(
        [jnp.concatenate([curv, norm], axis=1), jnp.concatenate([norm, eye], axis=1)]
    )
    step_ref[...] = step
    inv_ref[...] = inv
    curv_ref[...] = curv


def solve_second_kernel(gram_ref, step_ref, inv_ref, curv_ref, coef_ref):
    ens = step_ref.shape[0]
    norm = symmetric(gram_ref[:ens, :ens])
    cross = gram_ref[:ens, ens:]
    mixed = gram_ref[ens:, :ens]
    conj = mm(inv_ref[...], norm)
    coupled = mm(mixed, conj)
    quad = mm(conj, mm(curv_ref[...], conj), TN)
    curv = symmetric(cross + coupled + coupled.T + quad)
    (step,) = eliminate([jnp.concatenate([curv, norm], axis=1)])
    step0 = step_ref[...]
    keep = step0 + step + mm(conj, step)
    coef_ref[...] = jnp.concatenate([keep.T, -mm(step0, step).T], axis=1)


def solve_first(grams):
    ens = grams.shape[0]
    small = jax.ShapeDtypeStruct((ens, ens), f32)
    return pl.pallas_call(
        solve_first_kernel,
        out_shape=(small, small, small),
        in_specs=[vmem],
        out_specs=(vmem, vmem, vmem),
        name="solve_first",
    )(grams)


def solve_second(grams, step0, inv0, curv0):
    ens = step0.shape[0]
    return pl.pallas_call(
        solve_second_kernel,
        out_shape=jax.ShapeDtypeStruct((ens, 2 * ens), f32),
        in_specs=[vmem] * 4,
        out_specs=vmem,
        name="solve_second",
    )(grams, step0, inv0, curv0)


def add_columns(stack, owner, cols_ref):
    ens = cols_ref.shape[0]
    for c in range(2 * COLS_DEV // 256):
        slot = lax.broadcasted_iota(jnp.int32, (256, ROWS), 0) + c * 256
        hot = (slot == owner).astype(f32).astype(bf16)
        got = dot(stack, hot, NT)
        part = slice(c * 256, (c + 1) * 256)
        cols_ref[:, part] += got[:ens] + got[ens:]


def innov_columns_kernel(innov_ref, info_ref, cols_ref):
    cols_ref[...] = jnp.zeros_like(cols_ref)

    def one(g, carry):
        at = pl.ds(pl.multiple_of(g * ROWS, ROWS), ROWS)
        scale = info_ref[0:1, at] * info_ref[1:2, at]
        owner = info_ref[2:3, at].astype(jnp.int32)
        add_columns(jnp.concatenate(two(innov_ref[:, at] * scale), axis=0), owner, cols_ref)
        return carry

    lax.fori_loop(0, innov_ref.shape[1] // ROWS, one, 0)


def columns_kernel(info_ref, rank_ref, imga_ref, imgb_ref, back_ref, cols_ref):
    ens, own = back_ref.shape
    half = own // 2
    cols_ref[...] = jnp.zeros_like(cols_ref)
    for g in range(own // ROWS):
        at = slice(g * ROWS, (g + 1) * ROWS)
        rank = rank_ref[0:1, at].astype(jnp.int32)
        img_ref = imga_ref if g * ROWS < half else imgb_ref
        begin = (g * ROWS) % half
        lhs = jnp.concatenate(two(img_ref[:, begin : begin + ROWS]), axis=0)
        total = jnp.zeros((2 * ens, ROWS), f32)
        for c in range(ROWS // 256):
            slot = lax.broadcasted_iota(jnp.int32, (256, ROWS), 0) + c * 256
            place = (slot == rank).astype(f32).astype(bf16)
            total = total + dot(lhs[:, c * 256 : (c + 1) * 256], place)
        image = total[:ens] + total[ens:]
        back_ref[:, at] = image
        owner = info_ref[2:3, at].astype(jnp.int32)
        add_columns(jnp.concatenate(two(image * info_ref[0:1, at]), axis=0), owner, cols_ref)


def innov_columns_call(innov, info):
    ens, own = innov.shape
    return pl.pallas_call(
        innov_columns_kernel,
        out_shape=jax.ShapeDtypeStruct((ens, 2 * COLS_DEV), f32),
        in_specs=[vmem] * 2,
        out_specs=vmem,
        compiler_params=params(),
        cost_estimate=pl.CostEstimate(
            flops=2 * 256 * own * 2048, bytes_accessed=4 << 20, transcendentals=0
        ),
        name="innov_columns",
    )(innov, info)


def columns_call(info, rank, imga, imgb):
    ens, half = imga.shape
    return pl.pallas_call(
        columns_kernel,
        out_shape=(
            jax.ShapeDtypeStruct((ens, 2 * half), f32),
            jax.ShapeDtypeStruct((ens, 2 * COLS_DEV), f32),
        ),
        in_specs=[vmem] * 4,
        out_specs=(vmem, vmem),
        compiler_params=params(),
        cost_estimate=pl.CostEstimate(
            flops=2 * 256 * 2 * half * 3072, bytes_accessed=4 << 20, transcendentals=0
        ),
        name="columns",
    )(info, rank, imga, imgb)


def final_kernel(coef_ref, innov_ref, info_ref, back_ref, rc_ref, rin_ref, ic_ref, iin_ref, w_ref, inc_ref):
    coef = coef_ref[...]
    ens = coef.shape[0]
    own = innov_ref.shape[1]
    chunk = 1024
    first, second = coef[:, :ens], coef[:, ens:]
    for c in range(own // chunk):
        at = pl.ds(c * chunk, chunk)
        live = info_ref[1:2, at]
        w_ref[:, at] = combine(first, innov_ref[:, at] * live) + combine(second, back_ref[:, at])
    inc_ref[...] = combine(first, rc_ref[:, :COLS_DEV] + rin_ref[...]) + combine(
        second, ic_ref[:, :COLS_DEV] + iin_ref[...]
    )


def final_call(coef, innov, info, back, *cols):
    ens, own = innov.shape
    return pl.pallas_call(
        final_kernel,
        out_shape=(
            jax.ShapeDtypeStruct((ens, own), f32),
            jax.ShapeDtypeStruct((ens, COLS_DEV), f32),
        ),
        in_specs=[vmem] * 8,
        out_specs=(vmem, vmem),
        compiler_params=params(),
        name="final",
    )(coef, innov, info, back, *cols)


def block_bounds(key_ext, flags_ext, regions):
    wide = regions + 2 * REACH
    jkeys = key_ext.reshape(wide, ROWS // KB, KB)
    jmin = jkeys.min(axis=2)
    jmax = jnp.where(jkeys < 0.5 * DEAD, jkeys, -DEAD).max(axis=2)
    ikeys = key_ext.reshape(wide, ROWS // NB, NB)[REACH : REACH + regions]
    imin = ikeys.min(axis=2)
    imax = jnp.where(ikeys < 0.5 * DEAD, ikeys, -DEAD).max(axis=2)
    los, his = [], []
    ids = jnp.arange(ROWS // KB, dtype=jnp.int32)[None, None, :]
    for dh in range(2 * REACH + 1):
        lo_j = jmin[dh : dh + regions]
        hi_j = jmax[dh : dh + regions]
        d = dh - REACH
        if d == 0:
            flag = jnp.ones((regions,), jnp.bool_)
        elif d > 0:
            flag = flags_ext[d - 1, REACH : REACH + regions] > 0.5
        else:
            flag = flags_ext[-d - 1, REACH + d : REACH + d + regions] > 0.5
        near = (
            (hi_j[:, None, :] >= imin[:, :, None] - 1.001)
            & (lo_j[:, None, :] <= imax[:, :, None] + 1.001)
            & (imin[:, :, None] < 0.5 * DEAD)
            & flag[:, None, None]
        )
        los.append(jnp.where(near, ids, ROWS // KB).min(axis=2).reshape(-1))
        his.append(jnp.where(near, ids + 1, 0).max(axis=2).reshape(-1))
    return jnp.stack([jnp.concatenate(los), jnp.concatenate(his)])


def on_device(
    innovation,
    obs_along,
    obs_across,
    obs_scale,
    obs_error,
    obs_gain,
    pair_live,
    obs_count,
    col_owner,
):
    axes = ("reg", "col")
    regions = obs_count.shape[0]
    ens, own = innovation.shape
    live = (
        (jnp.arange(ROWS, dtype=jnp.int32)[None, :] < obs_count[:, None])
        .astype(f32)
        .reshape(own)
    )
    flags = jnp.repeat(pair_live.astype(f32).T, ROWS, axis=1)
    zero = jnp.zeros((own,), f32)
    meta = jnp.stack(
        [obs_along, obs_across, obs_scale * live, obs_error, flags[0], flags[1]]
        + [jnp.where(live > 0.5, obs_across, DEAD)]
        + [zero] * (META - 7)
    )
    total_cols = COLS_DEV * lax.axis_size(axes)
    local_col = (col_owner - lax.axis_index(axes) * COLS_DEV) % total_cols
    info = jnp.stack([obs_gain, live, local_col.astype(f32)] + [zero] * 5)

    first, last, rank = sort_call(innovation, meta)
    after = shift(first, -1)
    before = shift(last, 1)
    chunks = [before, first, last, after]
    innov_cols = innov_columns_call(innovation, info)
    innov_came = shift(innov_cols[:, COLS_DEV:], 1)
    keys = jnp.concatenate([c[ens + 6] for c in chunks])
    flags_ext = jnp.concatenate([c[ens + 4 : ens + 6, ::ROWS] for c in chunks], axis=1)
    bounds = block_bounds(keys, flags_ext, regions)

    imga, imgb, grams, *lists = first_call(bounds, chunks, ens, own)
    img_after = shift(imga, -1)
    img_before = shift(imgb, 1)
    step0, inv0, curv0 = solve_first(sum_all(grams, 0))
    back, img_cols = columns_call(info, rank, imga, imgb)
    img_came = shift(img_cols[:, COLS_DEV:], 1)
    grams = second_call(lists, step0, chunks, [img_before, imga, imgb, img_after], ens, own)
    coef = solve_second(sum_all(grams, 1), step0, inv0, curv0)
    return tuple(
        final_call(coef, innovation, info, back, innov_cols, innov_came, img_cols, img_came)
    )


def solution(mesh):
    one = P(("reg", "col"))
    in_specs = (P(None, ("reg", "col")), one, one, one, one, one, P(("reg", "col"), None), one, one)
    out_specs = (P(None, ("reg", "col")), P(None, ("reg", "col")))
    return jax.shard_map(
        on_device, mesh=mesh, in_specs=in_specs, out_specs=out_specs, check_vma=False
    )
```

profile of v0, /device:TPU:0, one launch (start us, length us, event | category | flops | bytes accessed | tf_op | source)
XLA Modules:
  0.0 161.0 jit_solution(14560071008148527700)
XLA Ops:
  0.6 0.7 convert_bitcast_fusion
  1.6 0.7 copy-done.6
  2.3 0.7 copy-done.8
  3.0 1.5 stack.48.meta_ref
  4.5 6.7 %sort_slots.1 = (f32[72,2048]{1,0:T(8,128)}, f32[72,2048]{1,0:T(8,128)}, f32[8,4096]{1,0:T(8,128)}) custom-call(f32[64,4096]{1,0:T(8,128)} %innov_ref.5, f32[16,4096]{1,0:T(8,128)} %stack.48.meta_ref), custom_call_target="tpu_custom_call" | custom-call | tf_op jit(solution)/shard_map/sort_slots/pallas_call | solution.py:98
  11.2 6.4 %collective-permute-start.1 = (f32[72,2048]{1,0:T(8,128)}, f32[72,2048]{1,0:T(8,128)S(1)}, u32[]{:S(2)}, u32[]{:S(2)}) collective-permute-start(f32[72,2048]{1,0:T(8,128)} %get-tuple-element.17.c1), channel_id=1, source_target_pairs={{1,0},{2,1},{3,2},{4,3},{5,4},{6,5},{7,6},{8,7},{9,8},{10,9},{11,1... | collective-permute-start | bytes 1769480 | tf_op jit(solution)/shard_map/ppermute | solution.py:33
  17.6 0.7 copy-done.11
  18.3 0.7 copy-done.10
  19.0 0.8 stack.55.info_ref
  19.8 8.1 %innov_columns.1.rc_ref = f32[64,2048]{1,0:T(8,128)} custom-call(f32[64,4096]{1,0:T(8,128)} %innov_ref.5, f32[8,4096]{1,0:T(8,128)} %stack.55.info_ref), custom_call_target="tpu_custom_call" | custom-call | flops 4294967296 | bytes 4194304 | tf_op jit(solution)/shard_map/innov_columns/pallas_call | solution.py:512
  27.9 1.0 slice.121
  28.9 0.8 slice.98
  29.7 0.8 slice.97
  30.6 0.1 fusion.7
  30.7 0.9 slice.107
  31.6 0.9 slice.103
  32.6 0.1 slice.102
  32.7 0.1 pad_maximum_fusion.3
  32.9 0.1 fusion
  33.1 0.1 and_and_fusion
  33.2 0.8 select_reduce_fusion.5
  34.0 0.1 reshape.153
  34.1 0.1 reshape.154
  34.1 0.1 reshape.155
  34.2 0.1 reshape.156
  34.3 0.1 reshape.157
  34.4 0.1 reshape.148
  34.5 0.1 reshape.149
  34.6 0.1 reshape.150
  34.6 0.1 reshape.151
  34.7 0.1 reshape.152
  34.8 0.1 concatenate.43
  34.9 0.1 concatenate.42
  35.0 0.6 pad_add_fusion.bounds_ref
  35.6 26.2 %operate_first.1 = (f32[64,2048]{1,0:T(8,128)}, f32[64,2048]{1,0:T(8,128)}, f32[64,128]{1,0:T(8,128)}, s32[1288]{0:T(1024)}, s32[322]{0:T(512)}, /*index=5*/s32[1]{0:T(128)}) custom-call(s32[2,160]{1,0:T(2,128)} %pad_add_fusion.bounds_ref, f32[72,2048]{1,0:T(8,128)} %copy-done, f32[72,2048]{1,0:T(8,128)} %get-tuple-element.17.c1, ...), custom_call_target="tpu_custom_call" | custom-call | tf_op jit(solution)/shard_map/operate_first/pallas_call | solution.py:313
  61.8 5.3 %collective-permute-start.3 = (f32[64,2048]{1,0:T(8,128)}, f32[64,2048]{1,0:T(8,128)S(1)}, u32[]{:S(2)}, u32[]{:S(2)}) collective-permute-start(f32[64,2048]{1,0:T(8,128)} %get-tuple-element.24.i1.imga_ref), channel_id=1, source_target_pairs={{1,0},{2,1},{3,2},{4,3},{5,4},{6,5},{7,6},{8,7},{9,8},{10,9},{11,1... | collective-permute-start | bytes 1572872 | tf_op jit(solution)/shard_map/ppermute | solution.py:33
  67.1 9.0 %columns.1 = (f32[64,4096]{1,0:T(8,128)}, f32[64,2048]{1,0:T(8,128)}) custom-call(f32[8,4096]{1,0:T(8,128)} %stack.55.info_ref, f32[8,4096]{1,0:T(8,128)} %get-tuple-element.27.rank_ref, f32[64,2048]{1,0:T(8,128)} %get-tuple-element.24.i1.imga_ref, f32[64,2048]{1,0:T(8,128)} %get-tuple-element.23.i2.imgb_ref), custom_call_target="tpu_custom_call" | custom-call | flops 6442450944 | bytes 4194304 | tf_op jit(solution)/shard_map/columns/pallas_call | solution.py:527
  76.2 1.0 slice.118
  77.2 17.3 %sum_all.2.gram_ref = f32[64,128]{1,0:T(8,128)} custom-call(f32[64,128]{1,0:T(8,128)} %get-tuple-element.21.x_ref), custom_call_target="tpu_custom_call" | custom-call | tf_op jit(solution)/shard_map/sum_all/pallas_call | solution.py:377
  94.5 7.2 %solve_first.1 = (f32[64,64]{1,0:T(8,128)}, f32[64,64]{1,0:T(8,128)}, f32[64,64]{1,0:T(8,128)}) custom-call(f32[64,128]{1,0:T(8,128)} %sum_all.2.gram_ref), custom_call_target="tpu_custom_call" | custom-call | tf_op jit(solution)/shard_map/solve_first/pallas_call | solution.py:446
  101.7 0.8 copy-done.2
  102.5 0.2 copy-done.3
  102.7 24.8 %operate_second.1.x_ref = f32[128,128]{1,0:T(8,128)} custom-call(s32[1288]{0:T(1024)} %get-tuple-element.18.list_ref, s32[322]{0:T(512)} %get-tuple-element.19.tile_ref, s32[1]{0:T(128)} %get-tuple-element.20.count_ref, f32[64,64]{1,0:T(8,128)} %get-tuple-element.22.step_ref, f32[72,2048]{1,0:T(8,128)} %copy-done, f32[72,2048]{1,0:T(8,128)} %get-tuple-element.17.c1, ...), custom_call_target="tpu_custom_call" | custom-call | tf_op jit(solution)/shard_map/operate_second/pallas_call | solution.py:332
  127.6 20.5 %sum_all.3.gram_ref = f32[128,128]{1,0:T(8,128)} custom-call(f32[128,128]{1,0:T(8,128)} %operate_second.1.x_ref), custom_call_target="tpu_custom_call" | custom-call | tf_op jit(solution)/shard_map/sum_all/pallas_call | solution.py:377
  148.1 8.2 %solve_second.1.coef_ref = f32[64,128]{1,0:T(8,128)} custom-call(f32[128,128]{1,0:T(8,128)} %sum_all.3.gram_ref, f32[64,64]{1,0:T(8,128)} %get-tuple-element.22.step_ref, f32[64,64]{1,0:T(8,128)} %get-tuple-element.25.inv_ref, f32[64,64]{1,0:T(8,128)} %get-tuple-element.26.curv_ref), custom_call_target="tpu_custom_call" | custom-call | tf_op jit(solution)/shard_map/solve_second/pallas_call | solution.py:457
  156.3 0.7 copy-done.4
  157.0 0.1 copy-done.5
  157.1 3.9 %final.1 = (f32[64,4096]{1,0:T(8,128)}, f32[64,1024]{1,0:T(8,128)}) custom-call(f32[64,128]{1,0:T(8,128)} %solve_second.1.coef_ref, f32[64,4096]{1,0:T(8,128)} %innov_ref.5, f32[8,4096]{1,0:T(8,128)} %stack.55.info_ref, f32[64,4096]{1,0:T(8,128)} %get-tuple-element.28.back_ref, f32[64,2048]{1,0:T(8,128)} %innov_columns.1.rc_ref, f32[64,1024]{1,0:T(8,128)} %copy-done.4, ...), custom_call_target="tpu_custom_call" | custom-call | tf_op jit(solution)/shard_map/final/pallas_call | solution.py:560
  (51 shorter events, 0.7 us)
Async XLA Ops:
  0.6 0.8 copy-start.12
  1.5 0.7 copy-start.6
  1.5 0.7 copy-start.7
  2.3 0.7 copy-start.8
  2.3 0.7 copy-start.9
  11.2 21.7 %collective-permute-start.1 = (f32[72,2048]{1,0:T(8,128)}, f32[72,2048]{1,0:T(8,128)S(1)}, u32[]{:S(2)}, u32[]{:S(2)}) collective-permute-start(f32[72,2048]{1,0:T(8,128)} %get-tuple-element.17.c1), channel_id=1, source_target_pairs={{1,0},{2,1},{3,2},{4,3},{5,4},{6,5},{7,6},{8,7},{9,8},{10,9},{11,1... | collective-permute-start | bytes 1769480 | tf_op jit(solution)/shard_map/ppermute | solution.py:33
  17.6 15.0 %collective-permute-start = (f32[72,2048]{1,0:T(8,128)}, f32[72,2048]{1,0:T(8,128)S(1)}, u32[]{:S(2)}, u32[]{:S(2)}) collective-permute-start(f32[72,2048]{1,0:T(8,128)} %get-tuple-element.16.c2), channel_id=1, source_target_pairs={{31,0},{0,1},{1,2},{2,3},{3,4},{4,5},{5,6},{6,7},{7,8},{8,9},{9,10... | collective-permute-start | bytes 1769480 | tf_op jit(solution)/shard_map/ppermute | solution.py:33
  17.6 0.7 copy-start.11
  18.3 0.7 copy-start.10
  28.8 127.5 %collective-permute-start.4 = (f32[64,1024]{1,0:T(8,128)S(1)}, f32[64,1024]{1,0:T(8,128)S(1)}, u32[]{:S(2)}, u32[]{:S(2)}) collective-permute-start(f32[64,1024]{1,0:T(8,128)S(1)} %slice.121), channel_id=1, source_target_pairs={{31,0},{0,1},{1,2},{2,3},{3,4},{4,5},{5,6},{6,7},{7,8},{8,9},{9,10... | collective-permute-start | bytes 786440 | tf_op jit(solution)/shard_map/ppermute | solution.py:33
  32.6 3.0 %copy-start = (f32[72,2048]{1,0:T(8,128)}, f32[72,2048]{1,0:T(8,128)S(1)}, u32[]{:S(2)}) copy-start(f32[72,2048]{1,0:T(8,128)S(1)} %collective-permute-done.c0) | copy-start | bytes 1769476
  32.8 2.7 %copy-start.1 = (f32[72,2048]{1,0:T(8,128)}, f32[72,2048]{1,0:T(8,128)S(1)}, u32[]{:S(2)}) copy-start(f32[72,2048]{1,0:T(8,128)S(1)} %collective-permute-done.1.c3) | copy-start | bytes 1769476
  61.7 40.0 %collective-permute-start.2 = (f32[64,2048]{1,0:T(8,128)}, f32[64,2048]{1,0:T(8,128)S(1)}, u32[]{:S(2)}, u32[]{:S(2)}) collective-permute-start(f32[64,2048]{1,0:T(8,128)} %get-tuple-element.23.i2.imgb_ref), channel_id=1, source_target_pairs={{31,0},{0,1},{1,2},{2,3},{3,4},{4,5},{5,6},{6,7},{7,8},{8,9},{9,10... | collective-permute-start | bytes 1572872 | tf_op jit(solution)/shard_map/ppermute | solution.py:33
  61.8 39.9 %collective-permute-start.3 = (f32[64,2048]{1,0:T(8,128)}, f32[64,2048]{1,0:T(8,128)S(1)}, u32[]{:S(2)}, u32[]{:S(2)}) collective-permute-start(f32[64,2048]{1,0:T(8,128)} %get-tuple-element.24.i1.imga_ref), channel_id=1, source_target_pairs={{1,0},{2,1},{3,2},{4,3},{5,4},{6,5},{7,6},{8,7},{9,8},{10,9},{11,1... | collective-permute-start | bytes 1572872 | tf_op jit(solution)/shard_map/ppermute | solution.py:33
  77.1 79.2 %collective-permute-start.5 = (f32[64,1024]{1,0:T(8,128)S(1)}, f32[64,1024]{1,0:T(8,128)S(1)}, u32[]{:S(2)}, u32[]{:S(2)}) collective-permute-start(f32[64,1024]{1,0:T(8,128)S(1)} %slice.118), channel_id=1, source_target_pairs={{31,0},{0,1},{1,2},{2,3},{3,4},{4,5},{5,6},{6,7},{7,8},{8,9},{9,10... | collective-permute-start | bytes 786440 | tf_op jit(solution)/shard_map/ppermute | solution.py:33
  101.7 0.8 copy-start.2
  101.7 1.0 copy-start.3
  156.3 0.7 copy-start.4
  156.3 0.8 copy-start.5
where the time goes:
time: 161 us
  Pallas kernels  132 us (82%)
  local copies, waits for them, and re-layouts  13.6 us (8%)
  starting transfers between devices  11.9 us (7%)
  other arithmetic  2.69 us (2%)
    pallas_call x2, Pallas kernels, sum_all(): pl.pallas_call(functools.partial(reduce_kernel, steps, n_col), out_shape=...  37.8 us
    pallas_call x1, Pallas kernels, first_call(): pl.pallas_call(first_kernel, out_shape=(half, half, jax.ShapeDtypeStruct(...  26.2 us
    pallas_call x1, Pallas kernels, second_call(): pl.pallas_call(second_kernel, out_shape=jax.ShapeDtypeStruct((2 * ens, 2...  24.8 us
    ppermute x6, starting transfers between devices, shift(): lax.ppermute(block, axis, [((i - distance) % n, i) for i in range(n)])  11.9 us
    pallas_call x1, Pallas kernels, columns_call(): pl.pallas_call(columns_kernel, out_shape=(jax.ShapeDtypeStruct((ens, 2 *...  9.03 us
    pallas_call x1, Pallas kernels, solve_second(): pl.pallas_call(solve_second_kernel, out_shape=jax.ShapeDtypeStruct((ens,...  8.23 us
    pallas_call x1, Pallas kernels, innov_columns_call(): pl.pallas_call(innov_columns_kernel, out_shape=jax.ShapeDtypeStruct((ens,...  8.06 us
    pallas_call x1, Pallas kernels, solve_first(): pl.pallas_call(solve_first_kernel, out_shape=(small, small, small), in_sp...  7.2 us
  transfers between devices with their start and end apart: 6, of which 0 were waited for; matrix products, arithmetic and copies ran while one was open for 6% of the time, Pallas kernels for 75%

commit v1 on v0

--- a/solution.py
+++ b/solution.py
@@ -61,7 +61,7 @@
     return pltpu.CompilerParams(vmem_limit_bytes=VMEM_LIMIT)
 
 
-def sort_kernel(innov_ref, meta_ref, first_ref, last_ref, rank_ref):
+def sort_kernel(innov_ref, meta_ref, first_ref, last_ref, rank_ref, own_ref):
     regions = innov_ref.shape[1] // ROWS
     kept = first_ref.shape[0]
     sub = lax.broadcasted_iota(jnp.int32, (ROWS, 128), 0)
@@ -89,7 +89,9 @@
             place = (slot == rank_i).astype(f32).astype(bf16)
             got = dot(lhs, place, NT)
             start = (g % (regions // 2)) * ROWS + c * 256
-            out_ref[:, start : start + 256] = (got[:n] + got[n : 2 * n] + got[2 * n :])[:kept]
+            got = (got[:n] + got[n : 2 * n] + got[2 * n :])[:kept]
+            out_ref[:, start : start + 256] = got
+            own_ref[:, g * ROWS + c * 256 : g * ROWS + (c + 1) * 256] = got[kept - 8 :]
 
 
 def sort_call(innov, meta):
@@ -97,9 +99,9 @@
     half = jax.ShapeDtypeStruct((ens + 8, n // 2), f32)
     return pl.pallas_call(
         sort_kernel,
-        out_shape=(half, half, jax.ShapeDtypeStruct((8, n), f32)),
+        out_shape=(half, half) + (jax.ShapeDtypeStruct((8, n), f32),) * 2,
         in_specs=[vmem, vmem],
-        out_specs=(vmem, vmem, vmem),
+        out_specs=(vmem,) * 4,
         compiler_params=params(),
         name="sort_slots",
     )(innov, meta)
@@ -340,50 +342,75 @@
     )(*lists, step, *chunks, *images)
 
 
+def flip(me, size):
+    return size * (1 - 2 * ((me // size) % 2))
+
+
+def exchange_steps(total):
+    bits = total.bit_length() - 1
+    steps = [[1]] if bits % 2 else []
+    for k in range(bits % 2, bits, 2):
+        steps.append([2**k, 2 ** (k + 1)])
+    return steps
+
+
 def reduce_kernel(steps, n_col, x_ref, out_ref, send, recv, send_sem, recv_sem):
     me = lax.axis_index("reg") * n_col + lax.axis_index("col")
     partners = []
-    for k in range(steps):
-        size = 2**k
-        other = me + size * (1 - 2 * ((me // size) % 2))
-        partners.append((other // n_col, other % n_col))
+    for sizes in steps:
+        others = [me + flip(me, size) for size in sizes]
+        if len(sizes) == 2:
+            others.append(others[0] + flip(me, sizes[1]))
+        partners.append([(other // n_col, other % n_col) for other in others])
     barrier = pltpu.get_barrier_semaphore()
-    for other in partners:
-        pl.semaphore_signal(
-            barrier, inc=1, device_id=other, device_id_type=pl.DeviceIdType.MESH
-        )
-    pl.semaphore_wait(barrier, steps)
+    for group in partners:
+        for other in group:
+            pl.semaphore_signal(
+                barrier, inc=1, device_id=other, device_id_type=pl.DeviceIdType.MESH
+            )
+    pl.semaphore_wait(barrier, sum(len(group) for group in partners))
     total = x_ref[...]
-    for k in range(steps):
+    slot = 0
+    for k, group in enumerate(partners):
         if k:
             send[k] = total
-        copy = pltpu.make_async_remote_copy(
-            src_ref=send.at[k] if k else x_ref,
-            dst_ref=recv.at[k],
-            send_sem=send_sem.at[k],
-            recv_sem=recv_sem.at[k],
-            device_id=partners[k],
-            device_id_type=pl.DeviceIdType.MESH,
-        )
-        copy.start()
-        copy.wait()
-        total = total + recv[k]
+        copies = []
+        for p, other in enumerate(group):
+            copies.append(
+                pltpu.make_async_remote_copy(
+                    src_ref=send.at[k] if k else x_ref,
+                    dst_ref=recv.at[slot + p],
+                    send_sem=send_sem.at[slot + p],
+                    recv_sem=recv_sem.at[slot + p],
+                    device_id=other,
+                    device_id_type=pl.DeviceIdType.MESH,
+                )
+            )
+        for copy in copies:
+            copy.start()
+        for copy in copies:
+            copy.wait()
+        total = total + recv[slot]
+        if len(group) == 3:
+            total = total + (recv[slot + 1] + recv[slot + 2])
+        slot += len(group)
     out_ref[...] = total
 
 
 def sum_all(x, which):
     n_col = lax.axis_size("col")
-    steps = (lax.axis_size("reg") * n_col).bit_length() - 1
+    steps = exchange_steps(lax.axis_size("reg") * n_col)
+    slots = sum(2 ** len(sizes) - 1 for sizes in steps)
     return pl.pallas_call(
         functools.partial(reduce_kernel, steps, n_col),
         out_shape=jax.ShapeDtypeStruct(x.shape, f32),
         in_specs=[vmem],
         out_specs=vmem,
         scratch_shapes=[
-            pltpu.VMEM((steps,) + x.shape, f32),
-            pltpu.VMEM((steps,) + x.shape, f32),
-            pltpu.SemaphoreType.DMA((steps,)),
-            pltpu.SemaphoreType.DMA((steps,)),
+            pltpu.VMEM((len(steps),) + x.shape, f32),
+            pltpu.VMEM((slots,) + x.shape, f32),
+            pltpu.SemaphoreType.DMA((slots,)),
+            pltpu.SemaphoreType.DMA((slots,)),
         ],
         compiler_params=pltpu.CompilerParams(collective_id=which, has_side_effects=True),
         name="sum_all",
@@ -631,14 +658,15 @@
     local_col = (col_owner - lax.axis_index(axes) * COLS_DEV) % total_cols
     info = jnp.stack([obs_gain, live, local_col.astype(f32)] + [zero] * 5)
 
-    first, last, rank = sort_call(innovation, meta)
+    first, last, rank, own_meta = sort_call(innovation, meta)
     after = shift(first, -1)
     before = shift(last, 1)
     chunks = [before, first, last, after]
     innov_cols = innov_columns_call(innovation, info)
     innov_came = shift(innov_cols[:, COLS_DEV:], 1)
-    keys = jnp.concatenate([c[ens + 6] for c in chunks])
-    flags_ext = jnp.concatenate([c[ens + 4 : ens + 6, ::ROWS] for c in chunks], axis=1)
+    metas = [before[ens:], own_meta, after[ens:]]
+    keys = jnp.concatenate([m[6] for m in metas])
+    flags_ext = jnp.concatenate([m[4:6, ::ROWS] for m in metas], axis=1)
     bounds = block_bounds(keys, flags_ext, regions)
 
     imga, imgb, grams, *lists = first_call(bounds, chunks, ens, own)

time: 161 us -> 156 us (0.969)
  Pallas kernels: 132 us -> 128 us
    pallas_call x2, Pallas kernels: 37.8 us -> 42.6 us  [sum_all(): pl.pallas_call(functools.partial(reduce_kernel, steps, n_col), out_shape=...]
    pallas_call x1, Pallas kernels: 26.2 us -> 21.8 us  [first_call(): pl.pallas_call(first_kernel, out_shape=(half, half, jax.ShapeDtypeStruct(...]
    pallas_call x1, Pallas kernels: 24.8 us -> 20.8 us  [second_call(): pl.pallas_call(second_kernel, out_shape=jax.ShapeDtypeStruct((2 * ens, 2...]
    slice x7 -> x6, local copies, waits for them, and re-layouts: 3.64 us -> 2.02 us  [the longest x2 1.08 us: on_device(): flags_ext = jnp.concatenate([m[4:6, ::ROWS] for m in metas], axis=1)]
  transfers between devices with their start and end apart: 6 -> 6, of which waited for: 0 -> 0; matrix products, arithmetic and copies ran while one was open for 6% -> 5% of each run, Pallas kernels for 75% -> 75%
where the time goes in v1:
time: 156 us
  Pallas kernels  128 us (82%)
  starting transfers between devices  12.2 us (8%)
  local copies, waits for them, and re-layouts  12 us (8%)
  other arithmetic  2.61 us (2%)
    pallas_call x2, Pallas kernels, sum_all(): pl.pallas_call(functools.partial(reduce_kernel, steps, n_col), out_shape=...  42.6 us
    pallas_call x1, Pallas kernels, first_call(): pl.pallas_call(first_kernel, out_shape=(half, half, jax.ShapeDtypeStruct(...  21.8 us
    pallas_call x1, Pallas kernels, second_call(): pl.pallas_call(second_kernel, out_shape=jax.ShapeDtypeStruct((2 * ens, 2...  20.8 us
    ppermute x6, starting transfers between devices, shift(): lax.ppermute(block, axis, [((i - distance) % n, i) for i in range(n)])  12.2 us
    pallas_call x1, Pallas kernels, columns_call(): pl.pallas_call(columns_kernel, out_shape=(jax.ShapeDtypeStruct((ens, 2 *...  9.03 us
    pallas_call x1, Pallas kernels, solve_second(): pl.pallas_call(solve_second_kernel, out_shape=jax.ShapeDtypeStruct((ens,...  8.24 us
    pallas_call x1, Pallas kernels, innov_columns_call(): pl.pallas_call(innov_columns_kernel, out_shape=jax.ShapeDtypeStruct((ens,...  8.06 us
    pallas_call x1, Pallas kernels, solve_first(): pl.pallas_call(solve_first_kernel, out_shape=(small, small, small), in_sp...  7.2 us
  transfers between devices with their start and end apart: 6, of which 0 were waited for; matrix products, arithmetic and copies ran while one was open for 5% of the time, Pallas kernels for 75%

profile of v1, /device:TPU:0, one launch (start us, length us, event | category | flops | bytes accessed | tf_op | source)
XLA Modules:
  0.0 156.0 jit_solution(17325346918918851862)
XLA Ops:
  0.6 0.7 convert_bitcast_fusion
  1.6 0.7 copy-done.6
  2.3 0.7 copy-done.8
  3.0 1.5 stack.48.meta_ref
  4.5 6.7 %sort_slots.1 = (f32[72,2048]{1,0:T(8,128)}, f32[72,2048]{1,0:T(8,128)}, f32[8,4096]{1,0:T(8,128)}, f32[8,4096]{1,0:T(8,128)}) custom-call(f32[64,4096]{1,0:T(8,128)} %innov_ref.5, f32[16,4096]{1,0:T(8,128)} %stack.48.meta_ref), custom_call_target="tpu_custom_call" | custom-call | tf_op jit(solution)/shard_map/sort_slots/pallas_call | solution.py:100
  11.2 6.4 %collective-permute-start.1 = (f32[72,2048]{1,0:T(8,128)}, f32[72,2048]{1,0:T(8,128)S(1)}, u32[]{:S(2)}, u32[]{:S(2)}) collective-permute-start(f32[72,2048]{1,0:T(8,128)} %get-tuple-element.19.c1), channel_id=1, source_target_pairs={{1,0},{2,1},{3,2},{4,3},{5,4},{6,5},{7,6},{8,7},{9,8},{10,9},{11,1... | collective-permute-start | bytes 1769480 | tf_op jit(solution)/shard_map/ppermute | solution.py:33
  17.7 0.7 copy-done.11
  18.4 0.7 copy-done.10
  19.1 0.8 stack.55.info_ref
  19.9 8.1 %innov_columns.1.rc_ref = f32[64,2048]{1,0:T(8,128)} custom-call(f32[64,4096]{1,0:T(8,128)} %innov_ref.5, f32[8,4096]{1,0:T(8,128)} %stack.55.info_ref), custom_call_target="tpu_custom_call" | custom-call | flops 4294967296 | bytes 4194304 | tf_op jit(solution)/shard_map/innov_columns/pallas_call | solution.py:539
  27.9 1.0 slice.120
  29.0 0.9 slice.95
  29.9 1.0 slice.102
  30.9 0.1 fusion.7
  31.1 0.1 fusion
  31.2 0.1 slice.101
  31.3 0.1 pad_maximum_fusion
  31.4 0.1 compare_bitcast_fusion.2
  31.5 0.1 and_and_fusion
  31.6 0.8 select_reduce_fusion.5
  32.4 0.1 reshape.144
  32.5 0.1 reshape.145
  32.5 0.1 reshape.146
  32.6 0.1 reshape.147
  32.7 0.1 reshape.148
  32.8 0.1 reshape.139
  32.9 0.1 reshape.140
  33.0 0.1 reshape.141
  33.0 0.1 reshape.142
  33.1 0.1 reshape.143
  33.2 0.1 concatenate.17
  33.3 0.1 concatenate.16
  33.4 0.6 pad_add_fusion.bounds_ref
  34.0 21.8 %operate_first.1 = (f32[64,2048]{1,0:T(8,128)}, f32[64,2048]{1,0:T(8,128)}, f32[64,128]{1,0:T(8,128)}, s32[1288]{0:T(1024)}, s32[322]{0:T(512)}, /*index=5*/s32[1]{0:T(128)}) custom-call(s32[2,160]{1,0:T(2,128)} %pad_add_fusion.bounds_ref, f32[72,2048]{1,0:T(8,128)} %copy-done, f32[72,2048]{1,0:T(8,128)} %get-tuple-element.19.c1, ...), custom_call_target="tpu_custom_call" | custom-call | tf_op jit(solution)/shard_map/operate_first/pallas_call | solution.py:315
  55.8 0.6 collective-permute-start.2
  56.3 5.1 %collective-permute-start.3 = (f32[64,2048]{1,0:T(8,128)}, f32[64,2048]{1,0:T(8,128)S(1)}, u32[]{:S(2)}, u32[]{:S(2)}) collective-permute-start(f32[64,2048]{1,0:T(8,128)} %get-tuple-element.26.i1.imga_ref), channel_id=1, source_target_pairs={{1,0},{2,1},{3,2},{4,3},{5,4},{6,5},{7,6},{8,7},{9,8},{10,9},{11,1... | collective-permute-start | bytes 1572872 | tf_op jit(solution)/shard_map/ppermute | solution.py:33
  61.4 9.0 %columns.1 = (f32[64,4096]{1,0:T(8,128)}, f32[64,2048]{1,0:T(8,128)}) custom-call(f32[8,4096]{1,0:T(8,128)} %stack.55.info_ref, f32[8,4096]{1,0:T(8,128)} %get-tuple-element.29.rank_ref, f32[64,2048]{1,0:T(8,128)} %get-tuple-element.26.i1.imga_ref, f32[64,2048]{1,0:T(8,128)} %get-tuple-element.25.i2.imgb_ref), custom_call_target="tpu_custom_call" | custom-call | flops 6442450944 | bytes 4194304 | tf_op jit(solution)/shard_map/columns/pallas_call | solution.py:554
  70.5 1.0 slice.116
  71.5 18.8 %sum_all.2.gram_ref = f32[64,128]{1,0:T(8,128)} custom-call(f32[64,128]{1,0:T(8,128)} %get-tuple-element.23.x_ref), custom_call_target="tpu_custom_call" | custom-call | tf_op jit(solution)/shard_map/sum_all/pallas_call | solution.py:404
  90.3 7.2 %solve_first.1 = (f32[64,64]{1,0:T(8,128)}, f32[64,64]{1,0:T(8,128)}, f32[64,64]{1,0:T(8,128)}) custom-call(f32[64,128]{1,0:T(8,128)} %sum_all.2.gram_ref), custom_call_target="tpu_custom_call" | custom-call | tf_op jit(solution)/shard_map/solve_first/pallas_call | solution.py:473
  97.5 0.8 copy-done.2
  98.3 0.2 copy-done.3
  98.5 20.8 %operate_second.1.x_ref = f32[128,128]{1,0:T(8,128)} custom-call(s32[1288]{0:T(1024)} %get-tuple-element.20.list_ref, s32[322]{0:T(512)} %get-tuple-element.21.tile_ref, s32[1]{0:T(128)} %get-tuple-element.22.count_ref, f32[64,64]{1,0:T(8,128)} %get-tuple-element.24.step_ref, f32[72,2048]{1,0:T(8,128)} %copy-done, f32[72,2048]{1,0:T(8,128)} %get-tuple-element.19.c1, ...), custom_call_target="tpu_custom_call" | custom-call | tf_op jit(solution)/shard_map/operate_second/pallas_call | solution.py:334
  119.3 23.8 %sum_all.3.gram_ref = f32[128,128]{1,0:T(8,128)} custom-call(f32[128,128]{1,0:T(8,128)} %operate_second.1.x_ref), custom_call_target="tpu_custom_call" | custom-call | tf_op jit(solution)/shard_map/sum_all/pallas_call | solution.py:404
  143.1 8.2 %solve_second.1.coef_ref = f32[64,128]{1,0:T(8,128)} custom-call(f32[128,128]{1,0:T(8,128)} %sum_all.3.gram_ref, f32[64,64]{1,0:T(8,128)} %get-tuple-element.24.step_ref, f32[64,64]{1,0:T(8,128)} %get-tuple-element.27.inv_ref, f32[64,64]{1,0:T(8,128)} %get-tuple-element.28.curv_ref), custom_call_target="tpu_custom_call" | custom-call | tf_op jit(solution)/shard_map/solve_second/pallas_call | solution.py:484
  151.4 0.7 copy-done.4
  152.1 0.1 copy-done.5
  152.2 3.9 %final.1 = (f32[64,4096]{1,0:T(8,128)}, f32[64,1024]{1,0:T(8,128)}) custom-call(f32[64,128]{1,0:T(8,128)} %solve_second.1.coef_ref, f32[64,4096]{1,0:T(8,128)} %innov_ref.5, f32[8,4096]{1,0:T(8,128)} %stack.55.info_ref, f32[64,4096]{1,0:T(8,128)} %get-tuple-element.30.back_ref, f32[64,2048]{1,0:T(8,128)} %innov_columns.1.rc_ref, f32[64,1024]{1,0:T(8,128)} %copy-done.4, ...), custom_call_target="tpu_custom_call" | custom-call | tf_op jit(solution)/shard_map/final/pallas_call | solution.py:587
  (48 shorter events, 0.5 us)
Async XLA Ops:
  0.6 0.8 copy-start.12
  1.5 0.7 copy-start.6
  1.5 0.7 copy-start.7
  2.3 0.7 copy-start.8
  2.3 0.7 copy-start.9
  11.2 19.8 %collective-permute-start.1 = (f32[72,2048]{1,0:T(8,128)}, f32[72,2048]{1,0:T(8,128)S(1)}, u32[]{:S(2)}, u32[]{:S(2)}) collective-permute-start(f32[72,2048]{1,0:T(8,128)} %get-tuple-element.19.c1), channel_id=1, source_target_pairs={{1,0},{2,1},{3,2},{4,3},{5,4},{6,5},{7,6},{8,7},{9,8},{10,9},{11,1... | collective-permute-start | bytes 1769480 | tf_op jit(solution)/shard_map/ppermute | solution.py:33
  17.6 13.4 %collective-permute-start = (f32[72,2048]{1,0:T(8,128)}, f32[72,2048]{1,0:T(8,128)S(1)}, u32[]{:S(2)}, u32[]{:S(2)}) collective-permute-start(f32[72,2048]{1,0:T(8,128)} %get-tuple-element.17.c2), channel_id=1, source_target_pairs={{31,0},{0,1},{1,2},{2,3},{3,4},{4,5},{5,6},{6,7},{7,8},{8,9},{9,10... | collective-permute-start | bytes 1769480 | tf_op jit(solution)/shard_map/ppermute | solution.py:33
  17.6 0.7 copy-start.11
  18.4 0.7 copy-start.10
  28.9 122.5 %collective-permute-start.4 = (f32[64,1024]{1,0:T(8,128)S(1)}, f32[64,1024]{1,0:T(8,128)S(1)}, u32[]{:S(2)}, u32[]{:S(2)}) collective-permute-start(f32[64,1024]{1,0:T(8,128)S(1)} %slice.120), channel_id=1, source_target_pairs={{31,0},{0,1},{1,2},{2,3},{3,4},{4,5},{5,6},{6,7},{7,8},{8,9},{9,10... | collective-permute-start | bytes 786440 | tf_op jit(solution)/shard_map/ppermute | solution.py:33
  31.0 2.9 %copy-start.1 = (f32[72,2048]{1,0:T(8,128)}, f32[72,2048]{1,0:T(8,128)S(1)}, u32[]{:S(2)}) copy-start(f32[72,2048]{1,0:T(8,128)S(1)} %collective-permute-done.1.c3) | copy-start | bytes 1769476
  31.1 2.9 %copy-start = (f32[72,2048]{1,0:T(8,128)}, f32[72,2048]{1,0:T(8,128)S(1)}, u32[]{:S(2)}) copy-start(f32[72,2048]{1,0:T(8,128)S(1)} %collective-permute-done.c0) | copy-start | bytes 1769476
  55.8 41.7 %collective-permute-start.2 = (f32[64,2048]{1,0:T(8,128)}, f32[64,2048]{1,0:T(8,128)S(1)}, u32[]{:S(2)}, u32[]{:S(2)}) collective-permute-start(f32[64,2048]{1,0:T(8,128)} %get-tuple-element.25.i2.imgb_ref), channel_id=1, source_target_pairs={{31,0},{0,1},{1,2},{2,3},{3,4},{4,5},{5,6},{6,7},{7,8},{8,9},{9,10... | collective-permute-start | bytes 1572872 | tf_op jit(solution)/shard_map/ppermute | solution.py:33
  56.3 41.1 %collective-permute-start.3 = (f32[64,2048]{1,0:T(8,128)}, f32[64,2048]{1,0:T(8,128)S(1)}, u32[]{:S(2)}, u32[]{:S(2)}) collective-permute-start(f32[64,2048]{1,0:T(8,128)} %get-tuple-element.26.i1.imga_ref), channel_id=1, source_target_pairs={{1,0},{2,1},{3,2},{4,3},{5,4},{6,5},{7,6},{8,7},{9,8},{10,9},{11,1... | collective-permute-start | bytes 1572872 | tf_op jit(solution)/shard_map/ppermute | solution.py:33
  71.4 79.9 %collective-permute-start.5 = (f32[64,1024]{1,0:T(8,128)S(1)}, f32[64,1024]{1,0:T(8,128)S(1)}, u32[]{:S(2)}, u32[]{:S(2)}) collective-permute-start(f32[64,1024]{1,0:T(8,128)S(1)} %slice.116), channel_id=1, source_target_pairs={{31,0},{0,1},{1,2},{2,3},{3,4},{4,5},{5,6},{6,7},{7,8},{8,9},{9,10... | collective-permute-start | bytes 786440 | tf_op jit(solution)/shard_map/ppermute | solution.py:33
  97.5 0.8 copy-start.2
  97.5 1.0 copy-start.3
  151.3 0.7 copy-start.4
  151.4 0.8 copy-start.5

commit v2 on v1

--- a/solution.py
+++ b/solution.py
@@ -13,7 +13,7 @@
 META = 16
 KB = 128
 NB = 128
-UNROLL = 4
+UNROLL = 2
 DEAD = 1e9
 VMEM_LIMIT = 60 * 1024 * 1024
 

time: 156 us -> 173 us (1.11)
  Pallas kernels: 128 us -> 144 us
    pallas_call x1, Pallas kernels: 21.8 us -> 28.2 us  [first_call(): pl.pallas_call(first_kernel, out_shape=(half, half, jax.ShapeDtypeStruct(...]
    pallas_call x1, Pallas kernels: 20.8 us -> 26.9 us  [second_call(): pl.pallas_call(second_kernel, out_shape=jax.ShapeDtypeStruct((2 * ens, 2...]
    pallas_call x2, Pallas kernels: 42.6 us -> 45.8 us  [sum_all(): pl.pallas_call(functools.partial(reduce_kernel, steps, n_col), out_shape=...]
  transfers between devices with their start and end apart: 6 -> 6, of which waited for: 0 -> 0; matrix products, arithmetic and copies ran while one was open for 5% -> 4% of each run, Pallas kernels for 75% -> 78%
where the time goes in v2:
time: 173 us; the launch traced here: 171 us
  Pallas kernels  144 us (83%)
  local copies, waits for them, and re-layouts  12 us (7%)
  starting transfers between devices  11.9 us (7%)
  other arithmetic  2.61 us (2%)
    pallas_call x2, Pallas kernels, sum_all(): pl.pallas_call(functools.partial(reduce_kernel, steps, n_col), out_shape=...  45.8 us
    pallas_call x1, Pallas kernels, first_call(): pl.pallas_call(first_kernel, out_shape=(half, half, jax.ShapeDtypeStruct(...  28.2 us
    pallas_call x1, Pallas kernels, second_call(): pl.pallas_call(second_kernel, out_shape=jax.ShapeDtypeStruct((2 * ens, 2...  26.9 us
    ppermute x6, starting transfers between devices, shift(): lax.ppermute(block, axis, [((i - distance) % n, i) for i in range(n)])  11.9 us
    pallas_call x1, Pallas kernels, columns_call(): pl.pallas_call(columns_kernel, out_shape=(jax.ShapeDtypeStruct((ens, 2 *...  9.03 us
    pallas_call x1, Pallas kernels, solve_second(): pl.pallas_call(solve_second_kernel, out_shape=jax.ShapeDtypeStruct((ens,...  8.23 us
    pallas_call x1, Pallas kernels, innov_columns_call(): pl.pallas_call(innov_columns_kernel, out_shape=jax.ShapeDtypeStruct((ens,...  8.06 us
    pallas_call x1, Pallas kernels, solve_first(): pl.pallas_call(solve_first_kernel, out_shape=(small, small, small), in_sp...  7.2 us
  transfers between devices with their start and end apart: 6, of which 0 were waited for; matrix products, arithmetic and copies ran while one was open for 4% of the time, Pallas kernels for 78%

profile of v2, /device:TPU:0, one launch (start us, length us, event | category | flops | bytes accessed | tf_op | source)
XLA Modules:
  0.0 171.5 jit_solution(16143336924338363895)
XLA Ops:
  0.6 0.7 convert_bitcast_fusion
  1.4 0.1 broadcast_bitcast_fusion
  1.6 0.7 copy-done.6
  2.3 0.7 copy-done.8
  3.0 1.5 stack.48.meta_ref
  4.5 6.7 %sort_slots.1 = (f32[72,2048]{1,0:T(8,128)}, f32[72,2048]{1,0:T(8,128)}, f32[8,4096]{1,0:T(8,128)}, f32[8,4096]{1,0:T(8,128)}) custom-call(f32[64,4096]{1,0:T(8,128)} %innov_ref.5, f32[16,4096]{1,0:T(8,128)} %stack.48.meta_ref), custom_call_target="tpu_custom_call" | custom-call | tf_op jit(solution)/shard_map/sort_slots/pallas_call | solution.py:100
  11.2 6.4 %collective-permute-start.1 = (f32[72,2048]{1,0:T(8,128)}, f32[72,2048]{1,0:T(8,128)S(1)}, u32[]{:S(2)}, u32[]{:S(2)}) collective-permute-start(f32[72,2048]{1,0:T(8,128)} %get-tuple-element.19.c1), channel_id=1, source_target_pairs={{1,0},{2,1},{3,2},{4,3},{5,4},{6,5},{7,6},{8,7},{9,8},{10,9},{11,1... | collective-permute-start | bytes 1769480 | tf_op jit(solution)/shard_map/ppermute | solution.py:33
  17.7 0.7 copy-done.11
  18.4 0.7 copy-done.10
  19.1 0.8 stack.55.info_ref
  19.9 8.1 %innov_columns.1.rc_ref = f32[64,2048]{1,0:T(8,128)} custom-call(f32[64,4096]{1,0:T(8,128)} %innov_ref.5, f32[8,4096]{1,0:T(8,128)} %stack.55.info_ref), custom_call_target="tpu_custom_call" | custom-call | flops 4294967296 | bytes 4194304 | tf_op jit(solution)/shard_map/innov_columns/pallas_call | solution.py:539
  27.9 1.0 slice.120
  29.0 0.9 slice.95
  29.9 1.0 slice.102
  30.9 0.1 fusion.7
  31.1 0.1 fusion
  31.2 0.1 slice.101
  31.3 0.1 pad_maximum_fusion
  31.4 0.1 compare_bitcast_fusion.2
  31.5 0.1 and_and_fusion
  31.6 0.8 select_reduce_fusion.5
  32.4 0.1 reshape.144
  32.5 0.1 reshape.145
  32.5 0.1 reshape.146
  32.6 0.1 reshape.147
  32.7 0.1 reshape.148
  32.8 0.1 reshape.139
  32.9 0.1 reshape.140
  33.0 0.1 reshape.141
  33.0 0.1 reshape.142
  33.1 0.1 reshape.143
  33.2 0.1 concatenate.17
  33.3 0.1 concatenate.16
  33.4 0.6 pad_add_fusion.bounds_ref
  34.0 28.2 %operate_first.1 = (f32[64,2048]{1,0:T(8,128)}, f32[64,2048]{1,0:T(8,128)}, f32[64,128]{1,0:T(8,128)}, s32[1284]{0:T(1024)}, s32[642]{0:T(1024)}, /*index=5*/s32[1]{0:T(128)}) custom-call(s32[2,160]{1,0:T(2,128)} %pad_add_fusion.bounds_ref, f32[72,2048]{1,0:T(8,128)} %copy-done, f32[72,2048]{1,0:T(8,128)} %get-tuple-element.19.c1, ...), custom_call_target="tpu_custom_call" | custom-call | tf_op jit(solution)/shard_map/operate_first/pallas_call | solution.py:315
  62.2 5.3 %collective-permute-start.3 = (f32[64,2048]{1,0:T(8,128)}, f32[64,2048]{1,0:T(8,128)S(1)}, u32[]{:S(2)}, u32[]{:S(2)}) collective-permute-start(f32[64,2048]{1,0:T(8,128)} %get-tuple-element.26.i1.imga_ref), channel_id=1, source_target_pairs={{1,0},{2,1},{3,2},{4,3},{5,4},{6,5},{7,6},{8,7},{9,8},{10,9},{11,1... | collective-permute-start | bytes 1572872 | tf_op jit(solution)/shard_map/ppermute | solution.py:33
  67.6 9.0 %columns.1 = (f32[64,4096]{1,0:T(8,128)}, f32[64,2048]{1,0:T(8,128)}) custom-call(f32[8,4096]{1,0:T(8,128)} %stack.55.info_ref, f32[8,4096]{1,0:T(8,128)} %get-tuple-element.29.rank_ref, f32[64,2048]{1,0:T(8,128)} %get-tuple-element.26.i1.imga_ref, f32[64,2048]{1,0:T(8,128)} %get-tuple-element.25.i2.imgb_ref), custom_call_target="tpu_custom_call" | custom-call | flops 6442450944 | bytes 4194304 | tf_op jit(solution)/shard_map/columns/pallas_call | solution.py:554
  76.6 1.0 slice.116
  77.6 21.3 %sum_all.2.gram_ref = f32[64,128]{1,0:T(8,128)} custom-call(f32[64,128]{1,0:T(8,128)} %get-tuple-element.23.x_ref), custom_call_target="tpu_custom_call" | custom-call | tf_op jit(solution)/shard_map/sum_all/pallas_call | solution.py:404
  99.0 7.2 %solve_first.1 = (f32[64,64]{1,0:T(8,128)}, f32[64,64]{1,0:T(8,128)}, f32[64,64]{1,0:T(8,128)}) custom-call(f32[64,128]{1,0:T(8,128)} %sum_all.2.gram_ref), custom_call_target="tpu_custom_call" | custom-call | tf_op jit(solution)/shard_map/solve_first/pallas_call | solution.py:473
  106.2 0.8 copy-done.2
  107.0 0.2 copy-done.3
  107.2 26.9 %operate_second.1.x_ref = f32[128,128]{1,0:T(8,128)} custom-call(s32[1284]{0:T(1024)} %get-tuple-element.20.list_ref, s32[642]{0:T(1024)} %get-tuple-element.21.tile_ref, s32[1]{0:T(128)} %get-tuple-element.22.count_ref, f32[64,64]{1,0:T(8,128)} %get-tuple-element.24.step_ref, f32[72,2048]{1,0:T(8,128)} %copy-done, f32[72,2048]{1,0:T(8,128)} %get-tuple-element.19.c1, ...), custom_call_target="tpu_custom_call" | custom-call | tf_op jit(solution)/shard_map/operate_second/pallas_call | solution.py:334
  134.0 24.5 %sum_all.3.gram_ref = f32[128,128]{1,0:T(8,128)} custom-call(f32[128,128]{1,0:T(8,128)} %operate_second.1.x_ref), custom_call_target="tpu_custom_call" | custom-call | tf_op jit(solution)/shard_map/sum_all/pallas_call | solution.py:404
  158.6 8.2 %solve_second.1.coef_ref = f32[64,128]{1,0:T(8,128)} custom-call(f32[128,128]{1,0:T(8,128)} %sum_all.3.gram_ref, f32[64,64]{1,0:T(8,128)} %get-tuple-element.24.step_ref, f32[64,64]{1,0:T(8,128)} %get-tuple-element.27.inv_ref, f32[64,64]{1,0:T(8,128)} %get-tuple-element.28.curv_ref), custom_call_target="tpu_custom_call" | custom-call | tf_op jit(solution)/shard_map/solve_second/pallas_call | solution.py:484
  166.8 0.7 copy-done.4
  167.5 0.1 copy-done.5
  167.6 3.9 %final.1 = (f32[64,4096]{1,0:T(8,128)}, f32[64,1024]{1,0:T(8,128)}) custom-call(f32[64,128]{1,0:T(8,128)} %solve_second.1.coef_ref, f32[64,4096]{1,0:T(8,128)} %innov_ref.5, f32[8,4096]{1,0:T(8,128)} %stack.55.info_ref, f32[64,4096]{1,0:T(8,128)} %get-tuple-element.30.back_ref, f32[64,2048]{1,0:T(8,128)} %innov_columns.1.rc_ref, f32[64,1024]{1,0:T(8,128)} %copy-done.4, ...), custom_call_target="tpu_custom_call" | custom-call | tf_op jit(solution)/shard_map/final/pallas_call | solution.py:587
  (48 shorter events, 0.4 us)
Async XLA Ops:
  0.6 0.8 copy-start.12
  1.5 0.7 copy-start.6
  1.5 0.7 copy-start.7
  2.3 0.7 copy-start.8
  2.3 0.7 copy-start.9
  11.2 19.8 %collective-permute-start.1 = (f32[72,2048]{1,0:T(8,128)}, f32[72,2048]{1,0:T(8,128)S(1)}, u32[]{:S(2)}, u32[]{:S(2)}) collective-permute-start(f32[72,2048]{1,0:T(8,128)} %get-tuple-element.19.c1), channel_id=1, source_target_pairs={{1,0},{2,1},{3,2},{4,3},{5,4},{6,5},{7,6},{8,7},{9,8},{10,9},{11,1... | collective-permute-start | bytes 1769480 | tf_op jit(solution)/shard_map/ppermute | solution.py:33
  17.6 13.4 %collective-permute-start = (f32[72,2048]{1,0:T(8,128)}, f32[72,2048]{1,0:T(8,128)S(1)}, u32[]{:S(2)}, u32[]{:S(2)}) collective-permute-start(f32[72,2048]{1,0:T(8,128)} %get-tuple-element.17.c2), channel_id=1, source_target_pairs={{31,0},{0,1},{1,2},{2,3},{3,4},{4,5},{5,6},{6,7},{7,8},{8,9},{9,10... | collective-permute-start | bytes 1769480 | tf_op jit(solution)/shard_map/ppermute | solution.py:33
  17.6 0.7 copy-start.11
  18.4 0.7 copy-start.10
  28.9 137.9 %collective-permute-start.4 = (f32[64,1024]{1,0:T(8,128)S(1)}, f32[64,1024]{1,0:T(8,128)S(1)}, u32[]{:S(2)}, u32[]{:S(2)}) collective-permute-start(f32[64,1024]{1,0:T(8,128)S(1)} %slice.120), channel_id=1, source_target_pairs={{31,0},{0,1},{1,2},{2,3},{3,4},{4,5},{5,6},{6,7},{7,8},{8,9},{9,10... | collective-permute-start | bytes 786440 | tf_op jit(solution)/shard_map/ppermute | solution.py:33
  31.0 2.9 %copy-start.1 = (f32[72,2048]{1,0:T(8,128)}, f32[72,2048]{1,0:T(8,128)S(1)}, u32[]{:S(2)}) copy-start(f32[72,2048]{1,0:T(8,128)S(1)} %collective-permute-done.1.c3) | copy-start | bytes 1769476
  31.1 2.9 %copy-start = (f32[72,2048]{1,0:T(8,128)}, f32[72,2048]{1,0:T(8,128)S(1)}, u32[]{:S(2)}) copy-start(f32[72,2048]{1,0:T(8,128)S(1)} %collective-permute-done.c0) | copy-start | bytes 1769476
  62.2 44.0 %collective-permute-start.2 = (f32[64,2048]{1,0:T(8,128)}, f32[64,2048]{1,0:T(8,128)S(1)}, u32[]{:S(2)}, u32[]{:S(2)}) collective-permute-start(f32[64,2048]{1,0:T(8,128)} %get-tuple-element.25.i2.imgb_ref), channel_id=1, source_target_pairs={{31,0},{0,1},{1,2},{2,3},{3,4},{4,5},{5,6},{6,7},{7,8},{8,9},{9,10... | collective-permute-start | bytes 1572872 | tf_op jit(solution)/shard_map/ppermute | solution.py:33
  62.2 44.0 %collective-permute-start.3 = (f32[64,2048]{1,0:T(8,128)}, f32[64,2048]{1,0:T(8,128)S(1)}, u32[]{:S(2)}, u32[]{:S(2)}) collective-permute-start(f32[64,2048]{1,0:T(8,128)} %get-tuple-element.26.i1.imga_ref), channel_id=1, source_target_pairs={{1,0},{2,1},{3,2},{4,3},{5,4},{6,5},{7,6},{8,7},{9,8},{10,9},{11,1... | collective-permute-start | bytes 1572872 | tf_op jit(solution)/shard_map/ppermute | solution.py:33
  77.6 89.2 %collective-permute-start.5 = (f32[64,1024]{1,0:T(8,128)S(1)}, f32[64,1024]{1,0:T(8,128)S(1)}, u32[]{:S(2)}, u32[]{:S(2)}) collective-permute-start(f32[64,1024]{1,0:T(8,128)S(1)} %slice.116), channel_id=1, source_target_pairs={{31,0},{0,1},{1,2},{2,3},{3,4},{4,5},{5,6},{6,7},{7,8},{8,9},{9,10... | collective-permute-start | bytes 786440 | tf_op jit(solution)/shard_map/ppermute | solution.py:33
  106.2 0.8 copy-start.2
  106.2 1.0 copy-start.3
  166.8 0.7 copy-start.4
  166.8 0.8 copy-start.5
